TPU v7x, 256 devices: a whole 4x4x8 slice. The times are simulated.
256 devices in a mesh: dp: 64 (over z, x, core), tensor: 4 (over y).
Axes of the slice: x: 4, y: 4, z: 8, core: 2. Of those that a mesh axis runs over, the one named last changes fastest.
Arguments:
- hidden: bfloat16 [8192, 4096], P('dp', 'tensor'), may hold values from -6 to 6
- grad_out: bfloat16 [8192, 4096], P('dp', 'tensor'), may hold values from -0.59765625 to 0.59765625
- query_weight: bfloat16 [4096, 4096], P(None, 'tensor'), may hold values from -0.09375 to 0.09375
- key_weight: bfloat16 [768, 4096], P(None, 'tensor'), may hold values from -0.21875 to 0.21875
- value_weight: bfloat16 [768, 4096], P(None, 'tensor'), may hold values from -0.21875 to 0.21875
- out_weight: bfloat16 [4096, 4096], P('tensor', 'dp'), may hold values from -0.75 to 0.75
- neighbour_states: bfloat16 [256, 128, 768], P('dp', None, 'tensor'), may hold values from -6 to 6
- block_owner: int32 [64, 4], P('dp'), may hold values from 0 to 63, as said below
- slot_target: int32 [64, 4], P('dp'), may hold values from 0 to 63, as said below
Outputs:
- cross_out: bfloat16 [8192, 4096], P('dp', 'tensor')
- grad_hidden: bfloat16 [8192, 4096], P('dp', 'tensor')
- grad_states: bfloat16 [256, 128, 768], P('dp', None, 'tensor')
Inputs may be any that keep to these rules, and one draw needn't show every extreme that they name: block_owner[d, t] = o exactly when slot_target[o, t] = d. The blocks 2k and 2k+1 of a dp index share their holder; the difference (holder - d) modulo the dp count is the same for every d, lies in 1 to 4, and differs between k. So a dp index holds exactly 2 blocks for each of 2 other indices. `slot_target`: the inverse map of block_owner, as stated there.
All inputs are finite; a program needn't handle non-finite values.
Results may differ from a plain program's by a relative error of at most 0.012.
Values may be sent and summed in bfloat16 or wider, within the bound.
No kernel may reach another device: no remote copies, remote signals or barrier semaphores. Data moves between devices by JAX's collectives and lax.ppermute only.
A program may use at most 128 MiB of HBM per device.

v0:
```python
import math
import jax
import jax.numpy as jnp
from jax import lax
from jax.sharding import PartitionSpec as P

HEADS = 32
SPAN = 64
K_NB = 2
CAP = 2
WINDOW = 4


def side_by_side(arrays, axis, dim, along):
    both = jnp.concatenate(arrays, axis=along)
    out, at, gathered = (lax.all_gather(both, axis, axis=dim, tiled=True), 0, [])
    for a in arrays:
        gathered.append(lax.slice_in_dim(out, at, at + a.shape[along], axis=along))
        at += a.shape[along]
    return tuple(gathered)


def shifted(x, axis, by):
    devices = lax.axis_size(axis)
    return lax.ppermute(x, axis, [(i, (i + by) % devices) for i in range(devices)])


def joined_along(tiles, dim):
    dims = list(tiles.shape[1:])
    dims[dim] *= tiles.shape[0]
    return jnp.moveaxis(tiles, 0, dim).reshape(dims)


def from_everyone(x, axis):
    copies = jnp.broadcast_to(x, (lax.axis_size(axis), *x.shape))
    return lax.all_to_all(copies, axis, split_axis=0, concat_axis=0, tiled=True)


def gathered_copies(x, axis, dim):
    return joined_along(from_everyone(x, axis), dim)


def split_up(x, dim, devices):
    dims = x.shape
    tiles = x.reshape(*dims[:dim], devices, dims[dim] // devices, *dims[dim + 1 :])
    return jnp.moveaxis(tiles, dim, 0)


def summed_on_arrival(x, axis, dim):
    tiles = split_up(x, dim, lax.axis_size(axis))
    arrived = lax.all_to_all(tiles, axis, split_axis=0, concat_axis=0, tiled=True)
    return arrived.astype(jnp.float32).sum(axis=0)


def sent_together(arrays, axis, dim, along):
    ends, at = ([], 0)
    for a in arrays[:-1]:
        at += a.shape[along]
        ends.append(at)
    both = jnp.concatenate(arrays, axis=along)
    return tuple(jnp.split(summed_on_arrival(both, axis, dim), ends, axis=along))


def contract_last(left, right):
    return lax.dot_general(
        left, right, (((1,), (1,)), ((), ())), preferred_element_type=jnp.float32
    )


def contract_first(left, right):
    return lax.dot_general(
        left, right, (((0,), (0,)), ((), ())), preferred_element_type=jnp.float32
    )


def shards(
    hidden,
    grad_out,
    query_weight,
    key_weight,
    value_weight,
    out_weight,
    neighbour_states,
    block_owner,
    slot_target,
):
    full_hidden, full_grad = side_by_side((hidden, grad_out), "tensor", 1, 0)
    out_gathered = lax.all_gather(out_weight, "dp", axis=1, tiled=True)
    dp_count = lax.axis_size("dp")
    my_index = lax.axis_index("dp")
    block_count, block_len, width_part = neighbour_states.shape
    block_ids = jnp.arange(block_count, dtype=jnp.int32)
    owner_gap = (block_owner[0] - my_index + dp_count) % dp_count
    target_gap = (my_index - slot_target[0] + dp_count) % dp_count
    pair_ids = jnp.arange(CAP, dtype=jnp.int32)
    flat_states = neighbour_states.reshape(block_count, block_len * width_part)
    delivered = jnp.zeros((block_count, block_len * width_part), jnp.float32)
    for offset in range(1, WINDOW + 1):
        send_table = (
            (target_gap[None, :] == offset) & ((block_ids % CAP)[None, :] == pair_ids[:, None])
        ).astype(jnp.bfloat16)
        receive_table = (
            (owner_gap[:, None] == offset) & ((block_ids % CAP)[:, None] == pair_ids[None, :])
        ).astype(jnp.bfloat16)
        outgoing = jnp.dot(send_table, flat_states, preferred_element_type=jnp.float32).astype(
            jnp.bfloat16
        )
        incoming = shifted(outgoing, "dp", -offset)
        delivered = delivered + jnp.dot(receive_table, incoming, preferred_element_type=jnp.float32)
    delivered = delivered.astype(jnp.bfloat16)
    neighbours = gathered_copies(
        delivered.reshape(block_count * block_len, width_part), "tensor", 1
    )
    query = jnp.dot(full_hidden, query_weight, preferred_element_type=jnp.float32).astype(
        jnp.bfloat16
    )
    key_rows = jnp.dot(neighbours, key_weight, preferred_element_type=jnp.float32).astype(
        jnp.bfloat16
    )
    value_rows = jnp.dot(neighbours, value_weight, preferred_element_type=jnp.float32).astype(
        jnp.bfloat16
    )
    local_heads = HEADS // lax.axis_size("tensor")
    head_size = query.shape[1] // local_heads
    span_count = query.shape[0] // SPAN
    score_scale = 1.0 / math.sqrt(head_size)
    query_heads = query.reshape(span_count, SPAN, local_heads, head_size)
    key_heads = key_rows.reshape(span_count, K_NB * block_len, local_heads, head_size)
    value_heads = value_rows.reshape(span_count, K_NB * block_len, local_heads, head_size)
    scores = (
        jnp.einsum("cqhd,ckhd->chqk", query_heads, key_heads, preferred_element_type=jnp.float32)
        * score_scale
    )
    highest = jnp.max(scores, axis=-1, keepdims=True)
    expanded = jnp.exp(scores - highest)
    probs = expanded / jnp.sum(expanded, axis=-1, keepdims=True)
    probs_low = probs.astype(jnp.bfloat16)
    attended = (
        jnp.einsum("chqk,ckhd->cqhd", probs_low, value_heads, preferred_element_type=jnp.float32)
        .astype(jnp.bfloat16)
        .reshape(query.shape)
    )
    out_partial = jnp.dot(attended, out_gathered, preferred_element_type=jnp.float32).astype(
        jnp.bfloat16
    )
    grad_attended = contract_last(full_grad, out_gathered).astype(jnp.bfloat16)
    grad_heads = grad_attended.reshape(query_heads.shape)
    grad_probs = jnp.einsum(
        "cqhd,ckhd->chqk", grad_heads, value_heads, preferred_element_type=jnp.float32
    )
    grad_scores = (
        probs * (grad_probs - jnp.sum(probs * grad_probs, axis=-1, keepdims=True)) * score_scale
    ).astype(jnp.bfloat16)
    grad_query = (
        jnp.einsum("chqk,ckhd->cqhd", grad_scores, key_heads, preferred_element_type=jnp.float32)
        .astype(jnp.bfloat16)
        .reshape(query.shape)
    )
    grad_key = (
        jnp.einsum("chqk,cqhd->ckhd", grad_scores, query_heads, preferred_element_type=jnp.float32)
        .astype(jnp.bfloat16)
        .reshape(key_rows.shape)
    )
    grad_value = (
        jnp.einsum("chqk,cqhd->ckhd", probs_low, grad_heads, preferred_element_type=jnp.float32)
        .astype(jnp.bfloat16)
        .reshape(value_rows.shape)
    )
    hidden_partial = contract_last(grad_query, query_weight).astype(jnp.bfloat16)
    states_partial = (
        contract_last(grad_key, key_weight) + contract_last(grad_value, value_weight)
    ).astype(jnp.bfloat16)
    out_summed, hidden_summed, states_summed = (
        *sent_together((out_partial, hidden_partial), "tensor", 1, 0),
        summed_on_arrival(states_partial, "tensor", 1),
    )
    cross_out = out_summed.astype(jnp.bfloat16)
    grad_hidden = hidden_summed.astype(jnp.bfloat16)
    grad_rows = states_summed.astype(jnp.bfloat16).reshape(block_count, block_len * width_part)
    grad_states = jnp.zeros((block_count, block_len * width_part), jnp.float32)
    for offset in range(1, WINDOW + 1):
        send_table = (
            (target_gap[None, :] == offset) & ((block_ids % CAP)[None, :] == pair_ids[:, None])
        ).astype(jnp.bfloat16)
        receive_table = (
            (owner_gap[:, None] == offset) & ((block_ids % CAP)[:, None] == pair_ids[None, :])
        ).astype(jnp.bfloat16)
        returning = contract_first(receive_table, grad_rows).astype(jnp.bfloat16)
        returned = shifted(returning, "dp", offset)
        grad_states = grad_states + contract_first(send_table, returned)
    grad_states = grad_states.astype(jnp.bfloat16)
    return (cross_out, grad_hidden, grad_states.reshape(block_count, block_len, width_part))


def solution(mesh):
    placed = (
        P("dp", "tensor"),
        P("dp", "tensor"),
        P(None, "tensor"),
        P(None, "tensor"),
        P(None, "tensor"),
        P("tensor", "dp"),
        P("dp", None, "tensor"),
        P("dp", None),
        P("dp", None),
    )
    return jax.shard_map(
        shards,
        mesh=mesh,
        in_specs=placed,
        out_specs=(P("dp", "tensor"), P("dp", "tensor"), P("dp", None, "tensor")),
        check_vma=False,
    )
```

profile of v0, /device:TPU:32, one launch (start us, length us, event | category | flops | bytes accessed | tf_op | source)
XLA Modules:
  0.0 235.4 jit_solution(10116544466631510508)
XLA Ops:
  7.2 2.0 pad_maximum_fusion.1
  9.3 0.7 all-gather.5.cloned.1.call-update
  10.0 1.1 copy.37
  11.1 0.3 reshape.114
  11.4 0.3 convolution_convert_fusion.7
  11.7 1.8 collective-permute-start
  13.5 0.3 convolution_convert_fusion.6
  13.8 0.9 collective-permute-start.1
  14.7 0.3 convolution_convert_fusion.5
  14.9 0.4 collective-permute-start.2
  15.4 0.3 convolution_convert_fusion.4
  15.7 8.1 %collective-permute-start.3 = (bf16[2,24576]{1,0:T(2,128)(2,1)S(1)}, bf16[2,24576]{1,0:T(2,128)(2,1)S(1)}, u32[]{:S(2)}, u32[]{:S(2)}) collective-permute-start(bf16[2,24576]{1,0:T(2,128)(2,1)S(1)} %convolution_convert_fusion.4), channel_id=1, source_target_pairs={{0,240},{4,244},{8,248},{12,252},{16,0},{20,4},{24,8},{28,12},{32,... | collective-permute-start | bytes 294920 | tf_op jit(solution)/shard_map/ppermute | solution.py:25
  23.8 2.5 %collective-permute-done.3 = bf16[2,24576]{1,0:T(2,128)(2,1)S(1)} collective-permute-done((bf16[2,24576]{1,0:T(2,128)(2,1)S(1)}, bf16[2,24576]{1,0:T(2,128)(2,1)S(1)}, u32[]{:S(2)}, u32[]{:S(2)}) %collective-permute-start.3) | collective-permute-done | bytes 98336 | tf_op jit(solution)/shard_map/ppermute | solution.py:25
  26.3 0.3 fusion.63
  26.6 0.3 fusion.60
  26.9 0.3 fusion.57
  27.3 0.4 fusion.6
  27.6 0.3 reshape.115
  28.1 25.8 %all_to_all.15 = bf16[4,512,192]{1,2,0:T(8,128)(2,1)S(1)} all-to-all(bf16[4,512,192]{1,2,0:T(8,128)(2,1)S(1)} %broadcast_in_dim.2), channel_id=1, replica_groups=mesh['dp'=64,'tensor'=4] {'tensor'}, dimensions={0} | all-to-all | bytes 1572864 | tf_op jit(solution)/shard_map/all_to_all | solution.py:36
  53.9 1.0 fusion.10
  54.9 0.3 copy.57
  55.2 1.1 copy-done.6
  56.3 1.0 fusion.9
  57.3 1.3 copy.58
  58.6 5.0 %fusion.18 = bf16[16,8,8,128]{3,1,2,0:T(8,128)(2,1)S(1)} fusion(bf16[4096,1024]{1,0:T(8,128)(2,1)} %param.11, bf16[256,4096]{1,0:T(8,128)(2,1)} %all-gather.3.cloned.1.call-done), kind=kOutput, calls=%fused_computation.42 | convolution fusion | flops 1073872896 | bytes 9699328 | tf_op jit(solution)/shard_map/dot_general | solution.py:114
  63.6 0.5 convolution_multiply_fusion
  64.1 1.0 copy-done.2
  65.1 1.2 fusion.115
  66.3 3.8 %fusion.20 = bf16[2,64,8,128]{3,1,2,0:T(8,128)(2,1)S(1)} fusion(bf16[2,256,8,128]{3,2,1,0:T(8,128)(2,1)} %bitcast.101, f32[2,8,64]{2,1,0:T(8,128)S(1)} %get-tuple-element.24, f32[2,8,64,256]{3,2,1,0:T(8,128)} %copy-done.2), kind=kOutput, calls=%fused_computation.44 | convolution fusion | flops 68027648 | bytes 2363392 | tf_op jit(solution)/shard_map/chqk,ckhd->cqhd/dot_general | solution.py:139
  70.3 69.9 %all-gather.5.cloned.1.call-done = bf16[1024,4096]{0,1:T(8,128)(2,1)} async-done(((bf16[1024,64]{0,1:T(8,128)(2,1)}), bf16[1024,4096]{0,1:T(8,128)(2,1)}) %all-gather.5.cloned.1.call-update) | async-done | bytes 8388624 | tf_op jit(solution)/shard_map/all_gather | solution.py:88
  140.2 5.0 %fusion.19 = bf16[16,8,8,128]{3,1,2,0:T(8,128)(2,1)S(1)} fusion(bf16[1024,4096]{0,1:T(8,128)(2,1)} %all-gather.5.cloned.1.call-done, bf16[256,4096]{1,0:T(8,128)(2,1)} %all-gather.3.cloned.1.call-done), kind=kOutput, calls=%fused_computation.43 | convolution fusion | flops 1073872896 | bytes 9699328 | tf_op jit(solution)/shard_map/dot_general | solution.py:65
  145.3 1.4 fusion.33
  146.7 4.7 %fusion.12 = bf16[2,256,8,128]{1,3,2,0:T(8,128)(2,1)} fusion(bf16[2,64,8,128]{3,2,1,0:T(8,128)(2,1)S(1)} %bitcast.108, f32[2,8,64]{2,1,0:T(8,128)S(1)} %get-tuple-element.24, f32[2,8,64,256]{3,2,1,0:T(8,128)} %copy-done.2), kind=kOutput, calls=%fused_computation.31 | convolution fusion | flops 68420864 | bytes 2363392 | tf_op jit(solution)/shard_map/chqk,cqhd->ckhd/dot_general | solution.py:165
  151.4 7.6 %fusion.21 = bf16[2,64,8,128]{3,1,2,0:T(8,128)(2,1)S(1)} fusion(f32[2,8,64,256]{3,2,1,0:T(8,128)} %fusion.33, bf16[2,256,8,128]{3,2,1,0:T(8,128)(2,1)S(1)} %bitcast.100, f32[2,8,64,256]{3,2,1,0:T(8,128)} %get-tuple-element.25, f32[2,8,64]{2,1,0:T(8,128)S(1)} %get-tuple-element.24), kind=kOutput, calls=%fused_computation.45 | convolution fusion | flops 69076224 | bytes 3411968 | tf_op jit(solution)/shard_map/chqk,ckhd->cqhd/dot_general | solution.py:155
  159.0 7.9 %fusion.11 = bf16[2,256,8,128]{1,3,2,0:T(8,128)(2,1)S(1)} fusion(f32[2,8,64,256]{3,2,1,0:T(8,128)} %fusion.33, bf16[2,64,8,128]{3,2,1,0:T(8,128)(2,1)S(1)} %bitcast.105, f32[2,8,64,256]{3,2,1,0:T(8,128)} %get-tuple-element.25, f32[2,8,64]{2,1,0:T(8,128)S(1)} %get-tuple-element.24), kind=kOutput, calls=%fused_computation.30 | convolution fusion | flops 69469440 | bytes 3411968 | tf_op jit(solution)/shard_map/chqk,cqhd->ckhd/dot_general | solution.py:160
  166.9 1.5 copy.49
  168.6 2.4 %copy.51 = bf16[2,256,8,128]{3,2,1,0:T(8,128)(2,1)} copy(bf16[2,256,8,128]{1,3,2,0:T(8,128)(2,1)} %fusion.12) | data formatting | bytes 2097152 | tf_op jit(solution)/shard_map/convert_element_type | solution.py:166
  171.0 2.4 %fusion.24 = f32[512,768]{1,0:T(8,128)S(1)} fusion(bf16[768,1024]{1,0:T(8,128)(2,1)S(1)} %copy-done, bf16[64,8,8,128]{3,2,1,0:T(8,128)(2,1)} %bitcast.109), kind=kOutput, calls=%fused_computation.48 | convolution fusion | flops 805306368 | bytes 4194304 | tf_op jit(solution)/shard_map/dot_general | solution.py:65
  173.4 1.0 add_convert_fusion
  174.4 1.2 copy.52
  175.7 4.4 %all-to-all-start.2 = ((bf16[4,512,192]{1,2,0:T(8,128)(2,1)}), bf16[4,512,192]{1,2,0:T(8,128)(2,1)S(1)}, u32[]{:S(2)}, u32[]{:S(2)}) async-start(bf16[4,512,192]{1,2,0:T(8,128)(2,1)} %bitcast.14), calls=%async_computation.2 | async-start | bytes 1572864 | tf_op jit(solution)/shard_map/all_to_all | solution.py:51
  180.1 6.3 %convolution_convert_fusion.8 = bf16[128,4096]{1,0:T(8,128)(2,1)S(1)} fusion(bf16[4096,1024]{1,0:T(8,128)(2,1)} %param.11, bf16[16,8,8,128]{3,2,1,0:T(8,128)(2,1)S(1)} %bitcast.106), kind=kOutput, calls=%fused_computation.18 | convolution fusion | flops 1074266112 | bytes 9699328 | tf_op jit(solution)/shard_map/dot_general | solution.py:65
  186.3 6.3 %convolution_convert_fusion.9 = bf16[128,4096]{1,0:T(8,128)(2,1)S(1)} fusion(bf16[1024,4096]{0,1:T(8,128)(2,1)} %all-gather.5.cloned.1.call-done, bf16[16,8,8,128]{3,2,1,0:T(8,128)(2,1)S(1)} %bitcast.103), kind=kOutput, calls=%fused_computation.19 | convolution fusion | flops 1074266112 | bytes 9699328 | tf_op jit(solution)/shard_map/dot_general | solution.py:143
  192.8 1.5 copy.97
  194.4 4.8 %all-to-all-start.1 = ((bf16[4,256,1024]{2,1,0:T(8,128)(2,1)}), bf16[4,256,1024]{2,1,0:T(8,128)(2,1)}, u32[]{:S(2)}, u32[]{:S(2)}) async-start(bf16[4,256,1024]{2,1,0:T(8,128)(2,1)} %bitcast.97), calls=%async_computation.1 | async-start | bytes 4194304 | tf_op jit(solution)/shard_map/all_to_all | solution.py:51
  199.5 0.3 reshape.127
  199.8 0.4 convolution_convert_fusion
  200.2 1.5 collective-permute-start.7
  201.7 0.4 convolution_convert_fusion.1
  202.1 0.4 convolution_convert_fusion.2
  202.4 0.4 convolution_convert_fusion.3
  202.9 0.2 collective-permute-start.5
  203.1 1.7 collective-permute-start.6
  204.9 2.5 %collective-permute-done.7 = bf16[2,24576]{1,0:T(2,128)(2,1)S(1)} collective-permute-done((bf16[2,24576]{1,0:T(2,128)(2,1)S(1)}, bf16[2,24576]{1,0:T(2,128)(2,1)S(1)}, u32[]{:S(2)}, u32[]{:S(2)}) %collective-permute-start.7) | collective-permute-done | bytes 98336 | tf_op jit(solution)/shard_map/ppermute | solution.py:25
  207.3 0.3 fusion.65
  207.7 3.7 %collective-permute-done.6 = bf16[2,24576]{1,0:T(2,128)(2,1)S(1)} collective-permute-done((bf16[2,24576]{1,0:T(2,128)(2,1)S(1)}, bf16[2,24576]{1,0:T(2,128)(2,1)S(1)}, u32[]{:S(2)}, u32[]{:S(2)}) %collective-permute-start.6) | collective-permute-done | bytes 98336 | tf_op jit(solution)/shard_map/ppermute | solution.py:25
  211.3 0.3 fusion.68
  211.8 0.3 fusion.71
  212.1 0.3 fusion.7
  212.5 0.3 reshape.128
  212.7 0.8 copy.54
  213.6 12.1 %all-to-all-done.1 = bf16[4,256,1024]{2,1,0:T(8,128)(2,1)} async-done(((bf16[4,256,1024]{2,1,0:T(8,128)(2,1)}), bf16[4,256,1024]{2,1,0:T(8,128)(2,1)}, u32[]{:S(2)}, u32[]{:S(2)}) %all-to-all-start.1) | async-done | bytes 2097184 | tf_op jit(solution)/shard_map/all_to_all | solution.py:51
  225.7 2.0 reduce.1
  227.7 0.8 fusion.114
  (39 shorter events, 1.5 us)
Async XLA Ops:
  7.2 46.7 %copy-start = (bf16[768,1024]{1,0:T(8,128)(2,1)S(1)}, bf16[768,1024]{1,0:T(8,128)(2,1)}, u32[]{:S(2)}) copy-start(bf16[768,1024]{1,0:T(8,128)(2,1)} %param.12) | copy-start | bytes 4718596
  7.2 4.2 %copy-start.4 = (s32[1,4]{1,0:T(1,128)S(1)}, s32[1,4]{1,0:T(1,128)}, u32[]{:S(2)}) copy-start(s32[1,4]{1,0:T(1,128)} %param.17) | copy-start | bytes 52
  7.2 16.6 %copy-start.5 = (s32[1,4]{1,0:T(1,128)S(1)}, s32[1,4]{1,0:T(1,128)}, u32[]{:S(2)}) copy-start(s32[1,4]{1,0:T(1,128)} %param.16) | copy-start | bytes 52
  7.2 51.4 %all-gather.3.cloned.1.call-start = ((), (), s32[]{:S(2)}) async-start(), calls=%async_computation.3 | async-start | bytes 2621440 | tf_op jit(solution)/shard_map/all_gather | solution.py:16
  9.3 130.9 %all-gather.5.cloned.1.call-start = ((), (), s32[]{:S(2)}) async-start(), calls=%async_computation.4 | async-start | bytes 8519680 | tf_op jit(solution)/shard_map/all_gather | solution.py:88
  11.7 15.6 %collective-permute-start = (bf16[2,24576]{1,0:T(2,128)(2,1)S(1)}, bf16[2,24576]{1,0:T(2,128)(2,1)S(1)}, u32[]{:S(2)}, u32[]{:S(2)}) collective-permute-start(bf16[2,24576]{1,0:T(2,128)(2,1)S(1)} %convolution_convert_fusion.7), channel_id=1, source_target_pairs={{0,252},{4,0},{8,4},{12,8},{16,12},{20,16},{24,20},{28,24},{32,28}... | collective-permute-start | bytes 294920 | tf_op jit(solution)/shard_map/ppermute | solution.py:25
  13.8 13.1 %collective-permute-start.1 = (bf16[2,24576]{1,0:T(2,128)(2,1)S(1)}, bf16[2,24576]{1,0:T(2,128)(2,1)S(1)}, u32[]{:S(2)}, u32[]{:S(2)}) collective-permute-start(bf16[2,24576]{1,0:T(2,128)(2,1)S(1)} %convolution_convert_fusion.6), channel_id=1, source_target_pairs={{0,248},{4,252},{8,0},{12,4},{16,8},{20,12},{24,16},{28,20},{32,24... | collective-permute-start | bytes 294920 | tf_op jit(solution)/shard_map/ppermute | solution.py:25
  14.9 11.6 %collective-permute-start.2 = (bf16[2,24576]{1,0:T(2,128)(2,1)S(1)}, bf16[2,24576]{1,0:T(2,128)(2,1)S(1)}, u32[]{:S(2)}, u32[]{:S(2)}) collective-permute-start(bf16[2,24576]{1,0:T(2,128)(2,1)S(1)} %convolution_convert_fusion.5), channel_id=1, source_target_pairs={{0,244},{4,248},{8,252},{12,0},{16,4},{20,8},{24,12},{28,16},{32,2... | collective-permute-start | bytes 294920 | tf_op jit(solution)/shard_map/ppermute | solution.py:25
  15.7 10.6 %collective-permute-start.3 = (bf16[2,24576]{1,0:T(2,128)(2,1)S(1)}, bf16[2,24576]{1,0:T(2,128)(2,1)S(1)}, u32[]{:S(2)}, u32[]{:S(2)}) collective-permute-start(bf16[2,24576]{1,0:T(2,128)(2,1)S(1)} %convolution_convert_fusion.4), channel_id=1, source_target_pairs={{0,240},{4,244},{8,248},{12,252},{16,0},{20,4},{24,8},{28,12},{32,... | collective-permute-start | bytes 294920 | tf_op jit(solution)/shard_map/ppermute | solution.py:25
  54.9 1.4 copy-start.6
  64.1 1.0 copy-start.2
  140.2 5.1 %copy-start.1 = (bf16[64,8,8,128]{3,2,1,0:T(8,128)(2,1)S(1)}, bf16[64,8,8,128]{3,2,1,0:T(8,128)(2,1)}, u32[]{:S(2)}) copy-start(bf16[64,8,8,128]{3,2,1,0:T(8,128)(2,1)} %copy.58) | copy-start | bytes 3145732
  171.0 2.4 %copy-start.3 = (bf16[2,256,8,128]{3,2,1,0:T(8,128)(2,1)S(1)}, bf16[2,256,8,128]{3,2,1,0:T(8,128)(2,1)}, u32[]{:S(2)}) copy-start(bf16[2,256,8,128]{3,2,1,0:T(8,128)(2,1)} %copy.51) | copy-start | bytes 3145732
  171.0 2.4 %copy-start.7 = (bf16[768,1024]{1,0:T(8,128)(2,1)S(1)}, bf16[768,1024]{1,0:T(8,128)(2,1)}, u32[]{:S(2)}) copy-start(bf16[768,1024]{1,0:T(8,128)(2,1)} %param.13) | copy-start | bytes 4718596
  175.7 18.7 %all-to-all-start.2 = ((bf16[4,512,192]{1,2,0:T(8,128)(2,1)}), bf16[4,512,192]{1,2,0:T(8,128)(2,1)S(1)}, u32[]{:S(2)}, u32[]{:S(2)}) async-start(bf16[4,512,192]{1,2,0:T(8,128)(2,1)} %bitcast.14), calls=%async_computation.2 | async-start | bytes 1572864 | tf_op jit(solution)/shard_map/all_to_all | solution.py:51
  194.4 31.3 %all-to-all-start.1 = ((bf16[4,256,1024]{2,1,0:T(8,128)(2,1)}), bf16[4,256,1024]{2,1,0:T(8,128)(2,1)}, u32[]{:S(2)}, u32[]{:S(2)}) async-start(bf16[4,256,1024]{2,1,0:T(8,128)(2,1)} %bitcast.97), calls=%async_computation.1 | async-start | bytes 4194304 | tf_op jit(solution)/shard_map/all_to_all | solution.py:51
  200.2 7.2 %collective-permute-start.7 = (bf16[2,24576]{1,0:T(2,128)(2,1)S(1)}, bf16[2,24576]{1,0:T(2,128)(2,1)S(1)}, u32[]{:S(2)}, u32[]{:S(2)}) collective-permute-start(bf16[2,24576]{1,0:T(2,128)(2,1)S(1)} %convolution_convert_fusion), channel_id=1, source_target_pairs={{0,16},{4,20},{8,24},{12,28},{16,32},{20,36},{24,40},{28,44},{32,4... | collective-permute-start | bytes 294920 | tf_op jit(solution)/shard_map/ppermute | solution.py:25
  202.8 9.3 %collective-permute-start.4 = (bf16[2,24576]{1,0:T(2,128)(2,1)S(1)}, bf16[2,24576]{1,0:T(2,128)(2,1)S(1)}, u32[]{:S(2)}, u32[]{:S(2)}) collective-permute-start(bf16[2,24576]{1,0:T(2,128)(2,1)S(1)} %convolution_convert_fusion.3), channel_id=1, source_target_pairs={{0,4},{4,8},{8,12},{12,16},{16,20},{20,24},{24,28},{28,32},{32,36}... | collective-permute-start | bytes 294920 | tf_op jit(solution)/shard_map/ppermute | solution.py:25
  202.9 8.9 %collective-permute-start.5 = (bf16[2,24576]{1,0:T(2,128)(2,1)S(1)}, bf16[2,24576]{1,0:T(2,128)(2,1)S(1)}, u32[]{:S(2)}, u32[]{:S(2)}) collective-permute-start(bf16[2,24576]{1,0:T(2,128)(2,1)S(1)} %convolution_convert_fusion.2), channel_id=1, source_target_pairs={{0,8},{4,12},{8,16},{12,20},{16,24},{20,28},{24,32},{28,36},{32,40... | collective-permute-start | bytes 294920 | tf_op jit(solution)/shard_map/ppermute | solution.py:25
  203.1 8.2 %collective-permute-start.6 = (bf16[2,24576]{1,0:T(2,128)(2,1)S(1)}, bf16[2,24576]{1,0:T(2,128)(2,1)S(1)}, u32[]{:S(2)}, u32[]{:S(2)}) collective-permute-start(bf16[2,24576]{1,0:T(2,128)(2,1)S(1)} %convolution_convert_fusion.1), channel_id=1, source_target_pairs={{0,12},{4,16},{8,20},{12,24},{16,28},{20,32},{24,36},{28,40},{32,4... | collective-permute-start | bytes 294920 | tf_op jit(solution)/shard_map/ppermute | solution.py:25
Sparse Core Ops, SparseCore 0:
  9.8 44.4 all-gather.2
  57.1 83.0 all-gather.4
where the time goes:
time: 236 us; the launch traced here: 235 us
  waiting for transfers between devices  91.5 us (39%)
  matrix products  59 us (25%)
  blocking collectives  25.8 us (11%)
  starting transfers between devices  24.1 us (10%)
  local copies, waits for them, and re-layouts  15 us (6%)
  between operations  14.5 us (6%)
  other arithmetic  5.61 us (2%)
    all_gather x1, waiting for transfers between devices, shards(): out_gathered = lax.all_gather(out_weight, 'dp', axis=1, tiled=True)  69.9 us
    all_to_all x1, blocking collectives, from_everyone(): return lax.all_to_all(copies, axis, split_axis=0, concat_axis=0, tiled=True)  25.8 us
    ppermute x8, starting transfers between devices, shifted(): lax.ppermute(x, axis, [(i, (i + by) % devices) for i in range(devices)])  14.8 us
    dot_general x4, matrix products, contract_last(): lax.dot_general(left, right, (((1,), (1,)), ((), ())), preferred_element_...  14.7 us
    all_to_all x2, waiting for transfers between devices, summed_on_arrival(): lax.all_to_all(tiles, axis, split_axis=0, concat_axis=0, tiled=True)  12.1 us
    all_to_all x2, starting transfers between devices, summed_on_arrival(): lax.all_to_all(tiles, axis, split_axis=0, concat_axis=0, tiled=True)  9.18 us
    ppermute x8, waiting for transfers between devices, shifted(): lax.ppermute(x, axis, [(i, (i + by) % devices) for i in range(devices)])  8.77 us
    dot_general x1, matrix products, shards(): jnp.einsum('chqk,cqhd->ckhd', grad_scores, query_heads, preferred_element...  7.92 us
  transfers between devices with their start and end apart: 12, of which 6 were waited for; matrix products, arithmetic and copies ran while one was open for 16% of the time, Pallas kernels for 0%

commit v1 on v0

--- a/solution.py
+++ b/solution.py
@@ -85,7 +85,8 @@
     slot_target,
 ):
     full_hidden, full_grad = side_by_side((hidden, grad_out), "tensor", 1, 0)
-    out_gathered = lax.all_gather(out_weight, "dp", axis=1, tiled=True)
+    sent = jnp.stack([out_weight] * lax.axis_size("dp"))
+    out_gathered = jnp.concatenate(lax.all_to_all(sent, "dp", 0, 0), axis=1)
     dp_count = lax.axis_size("dp")
     my_index = lax.axis_index("dp")
     block_count, block_len, width_part = neighbour_states.shape

time: 236 us -> 341 us (1.44)
  waiting for transfers between devices: 91.5 us -> 186 us
  starting transfers between devices: 24.1 us -> 37 us
  blocking collectives: 25.8 us -> 14.6 us
  matrix products: 59 us -> 64.7 us
    all_to_all x0 -> x1, waiting for transfers between devices: none -> 139 us  [shards(): out_gathered = jnp.concatenate(lax.all_to_all(sent, 'dp', 0, 0), axis=1)]
    all_gather x1 -> x0, waiting for transfers between devices: 69.9 us -> none  [shards(): out_gathered = lax.all_gather(out_weight, 'dp', axis=1, tiled=True)]
    all_gather x1, waiting for transfers between devices: 0.01 us -> 29.3 us  [side_by_side(): lax.all_gather(both, axis, axis=dim, tiled=True)]
    all_to_all x1, blocking collectives: 25.8 us -> 14.6 us  [from_everyone(): return lax.all_to_all(copies, axis, split_axis=0, concat_axis=0, tiled=True)]
    all_to_all x0 -> x1, starting transfers between devices: none -> 10.8 us  [shards(): out_gathered = jnp.concatenate(lax.all_to_all(sent, 'dp', 0, 0), axis=1)]
    another operation x0 -> x1, local copies, waits for them, and re-layouts: none -> 4.29 us  [shards(): sent = jnp.stack([out_weight] * lax.axis_size('dp'))]
  transfers between devices with their start and end apart: 12 -> 12, of which waited for: 6 -> 8; matrix products, arithmetic and copies ran while one was open for 16% -> 11% of each run, Pallas kernels for 0% -> 0%
where the time goes in v1:
time: 341 us; the launch traced here: 340 us
  waiting for transfers between devices  186 us (55%)
  matrix products  64.7 us (19%)
  starting transfers between devices  37 us (11%)
  local copies, waits for them, and re-layouts  18.4 us (5%)
  blocking collectives  14.6 us (4%)
  between operations  14.5 us (4%)
  other arithmetic  5.23 us (2%)
    all_to_all x1, waiting for transfers between devices, shards(): out_gathered = jnp.concatenate(lax.all_to_all(sent, 'dp', 0, 0), axis=1)  139 us
    all_gather x1, waiting for transfers between devices, side_by_side(): lax.all_gather(both, axis, axis=dim, tiled=True)  29.3 us
    dot_general x4, matrix products, contract_last(): lax.dot_general(left, right, (((1,), (1,)), ((), ())), preferred_element_...  18.1 us
    ppermute x8, starting transfers between devices, shifted(): lax.ppermute(x, axis, [(i, (i + by) % devices) for i in range(devices)])  17.7 us
    all_to_all x1, blocking collectives, from_everyone(): return lax.all_to_all(copies, axis, split_axis=0, concat_axis=0, tiled=True)  14.6 us
    all_to_all x1, starting transfers between devices, shards(): out_gathered = jnp.concatenate(lax.all_to_all(sent, 'dp', 0, 0), axis=1)  10.8 us
    all_to_all x2, waiting for transfers between devices, summed_on_arrival(): lax.all_to_all(tiles, axis, split_axis=0, concat_axis=0, tiled=True)  10.6 us
    dot_general x1, matrix products, shards(): jnp.einsum('chqk,cqhd->ckhd', grad_scores, query_heads, preferred_element...  8.95 us
  transfers between devices with their start and end apart: 12, of which 8 were waited for; matrix products, arithmetic and copies ran while one was open for 11% of the time, Pallas kernels for 0%

profile of v1, /device:TPU:32, one launch (start us, length us, event | category | flops | bytes accessed | tf_op | source)
XLA Modules:
  0.0 340.3 jit_solution(2943615281487932775)
XLA Ops:
  7.2 0.8 compare_bitcast_fusion.3
  8.0 1.1 copy.38
  9.1 0.3 reshape.122
  9.6 2.4 collective-permute-start.1
  12.4 0.3 convolution_convert_fusion.4
  12.6 8.0 %collective-permute-start.3 = (bf16[2,24576]{1,0:T(2,128)(2,1)S(1)}, bf16[2,24576]{1,0:T(2,128)(2,1)S(1)}, u32[]{:S(2)}, u32[]{:S(2)}) collective-permute-start(bf16[2,24576]{1,0:T(2,128)(2,1)S(1)} %convolution_convert_fusion.4), channel_id=1, source_target_pairs={{0,240},{4,244},{8,248},{12,252},{16,0},{20,4},{24,8},{28,12},{32,... | collective-permute-start | bytes 294920 | tf_op jit(solution)/shard_map/ppermute | solution.py:25
  20.9 1.5 collective-permute-start
  22.5 0.3 fusion.57
  22.8 0.3 fusion.60
  23.2 0.3 fusion.63
  23.5 1.2 collective-permute-done
  24.7 0.4 fusion.6
  25.0 0.3 reshape.123
  25.5 14.6 %all_to_all.20 = bf16[4,512,192]{1,2,0:T(8,128)(2,1)S(1)} all-to-all(bf16[4,512,192]{1,2,0:T(8,128)(2,1)S(1)} %broadcast_in_dim.2), channel_id=1, replica_groups=mesh['dp'=64,'tensor'=4] {'tensor'}, dimensions={0} | all-to-all | bytes 1572864 | tf_op jit(solution)/shard_map/all_to_all | solution.py:36
  40.1 4.3 %stack.2 = bf16[64,1024,64]{1,2,0:T(8,128)(2,1)} broadcast(bf16[1024,64]{0,1:T(8,128)(2,1)S(1)} %copy-done.6), dimensions={1,2} | broadcast | bytes 8519680 | tf_op jit(solution)/shard_map/stack | solution.py:88
  44.4 10.8 %all-to-all-start.1 = ((bf16[64,1024,64]{1,2,0:T(8,128)(2,1)}), bf16[64,1024,64]{1,2,0:T(8,128)(2,1)}, u32[]{:S(2)}, u32[]{:S(2)}) async-start(bf16[64,1024,64]{1,2,0:T(8,128)(2,1)} %stack.2), calls=%async_computation.1 | async-start | bytes 16777216 | tf_op jit(solution)/shard_map/all_to_all | solution.py:89
  55.5 0.8 pad_maximum_fusion.1
  56.3 2.4 fusion.9
  58.8 1.2 copy.59
  60.0 1.0 fusion.10
  61.0 0.3 copy.58
  61.3 29.3 %all-gather.2.cloned.1.call-done = bf16[256,4096]{1,0:T(8,128)(2,1)} async-done(((bf16[256,1024]{1,0:T(8,128)(2,1)}), bf16[256,4096]{1,0:T(8,128)(2,1)}) %all-gather.2.cloned.1.call-update) | async-done | bytes 2097168 | tf_op jit(solution)/shard_map/all_gather | solution.py:16
  90.6 5.0 %fusion.18 = bf16[16,8,8,128]{3,1,2,0:T(8,128)(2,1)S(1)} fusion(bf16[4096,1024]{1,0:T(8,128)(2,1)} %param.11, bf16[256,4096]{1,0:T(8,128)(2,1)} %all-gather.2.cloned.1.call-done), kind=kOutput, calls=%fused_computation.42 | convolution fusion | flops 1073872896 | bytes 9699328 | tf_op jit(solution)/shard_map/dot_general | solution.py:115
  95.7 0.5 convolution_multiply_fusion
  96.2 1.0 copy-done.2
  97.1 1.2 fusion.115
  98.3 3.7 %fusion.20 = bf16[2,64,8,128]{3,1,2,0:T(8,128)(2,1)S(1)} fusion(bf16[2,256,8,128]{3,2,1,0:T(8,128)(2,1)} %bitcast.104, f32[2,8,64]{2,1,0:T(8,128)S(1)} %get-tuple-element.24, f32[2,8,64,256]{3,2,1,0:T(8,128)} %copy-done.2), kind=kOutput, calls=%fused_computation.44 | convolution fusion | flops 68027648 | bytes 2363392 | tf_op jit(solution)/shard_map/chqk,ckhd->cqhd/dot_general | solution.py:140
  102.2 139.3 %all-to-all-done.1 = bf16[64,1024,64]{1,2,0:T(8,128)(2,1)} async-done(((bf16[64,1024,64]{1,2,0:T(8,128)(2,1)}), bf16[64,1024,64]{1,2,0:T(8,128)(2,1)}, u32[]{:S(2)}, u32[]{:S(2)}) %all-to-all-start.1) | async-done | bytes 8388640 | tf_op jit(solution)/shard_map/all_to_all | solution.py:89
  241.5 5.0 %fusion.19 = bf16[16,8,8,128]{3,1,2,0:T(8,128)(2,1)S(1)} fusion(bf16[1024,4096]{0,1:T(8,128)(2,1)} %bitcast.10, bf16[256,4096]{1,0:T(8,128)(2,1)} %all-gather.2.cloned.1.call-done), kind=kOutput, calls=%fused_computation.43 | convolution fusion | flops 1073872896 | bytes 9699328 | tf_op jit(solution)/shard_map/dot_general | solution.py:65
  246.7 1.5 fusion.33
  248.2 4.6 %fusion.12 = bf16[2,256,8,128]{1,3,2,0:T(8,128)(2,1)} fusion(bf16[2,64,8,128]{3,2,1,0:T(8,128)(2,1)S(1)} %bitcast.110, f32[2,8,64]{2,1,0:T(8,128)S(1)} %get-tuple-element.24, f32[2,8,64,256]{3,2,1,0:T(8,128)} %copy-done.2), kind=kOutput, calls=%fused_computation.31 | convolution fusion | flops 68420864 | bytes 2363392 | tf_op jit(solution)/shard_map/chqk,cqhd->ckhd/dot_general | solution.py:166
  252.8 9.0 %fusion.11 = bf16[2,256,8,128]{1,3,2,0:T(8,128)(2,1)} fusion(f32[2,8,64,256]{3,2,1,0:T(8,128)} %fusion.33, bf16[2,64,8,128]{3,2,1,0:T(8,128)(2,1)S(1)} %bitcast.108, f32[2,8,64,256]{3,2,1,0:T(8,128)} %get-tuple-element.25, f32[2,8,64]{2,1,0:T(8,128)S(1)} %get-tuple-element.24), kind=kOutput, calls=%fused_computation.30 | convolution fusion | flops 69469440 | bytes 3411968 | tf_op jit(solution)/shard_map/chqk,cqhd->ckhd/dot_general | solution.py:161
  261.7 7.7 %fusion.21 = bf16[2,64,8,128]{3,1,2,0:T(8,128)(2,1)S(1)} fusion(f32[2,8,64,256]{3,2,1,0:T(8,128)} %fusion.33, bf16[2,256,8,128]{3,2,1,0:T(8,128)(2,1)S(1)} %bitcast.103, f32[2,8,64,256]{3,2,1,0:T(8,128)} %get-tuple-element.25, f32[2,8,64]{2,1,0:T(8,128)S(1)} %get-tuple-element.24), kind=kOutput, calls=%fused_computation.45 | convolution fusion | flops 69076224 | bytes 3411968 | tf_op jit(solution)/shard_map/chqk,ckhd->cqhd/dot_general | solution.py:156
  269.4 2.7 copy.50
  272.1 3.5 %fusion.24 = f32[512,768]{1,0:T(8,128)} fusion(bf16[768,1024]{1,0:T(8,128)(2,1)S(1)} %copy-done, bf16[64,8,8,128]{3,2,1,0:T(8,128)(2,1)} %bitcast.113), kind=kOutput, calls=%fused_computation.48 | convolution fusion | flops 805306368 | bytes 4194304 | tf_op jit(solution)/shard_map/dot_general | solution.py:65
  275.7 1.5 copy.52
  277.1 3.2 add_convert_fusion
  280.4 1.2 copy.53
  281.6 3.5 %all-to-all-start.3 = ((bf16[4,512,192]{1,2,0:T(8,128)(2,1)}), bf16[4,512,192]{1,2,0:T(8,128)(2,1)S(1)}, u32[]{:S(2)}, u32[]{:S(2)}) async-start(bf16[4,512,192]{1,2,0:T(8,128)(2,1)} %bitcast.17), calls=%async_computation.3 | async-start | bytes 1572864 | tf_op jit(solution)/shard_map/all_to_all | solution.py:51
  285.1 6.3 %convolution_convert_fusion.9 = bf16[128,4096]{1,0:T(8,128)(2,1)S(1)} fusion(bf16[1024,4096]{0,1:T(8,128)(2,1)} %bitcast.10, bf16[16,8,8,128]{3,2,1,0:T(8,128)(2,1)S(1)} %bitcast.106), kind=kOutput, calls=%fused_computation.19 | convolution fusion | flops 1074266112 | bytes 9699328 | tf_op jit(solution)/shard_map/dot_general | solution.py:144
  291.5 6.3 %convolution_convert_fusion.8 = bf16[128,4096]{1,0:T(8,128)(2,1)S(1)} fusion(bf16[4096,1024]{1,0:T(8,128)(2,1)} %param.11, bf16[16,8,8,128]{3,2,1,0:T(8,128)(2,1)S(1)} %bitcast.111), kind=kOutput, calls=%fused_computation.18 | convolution fusion | flops 1074266112 | bytes 9699328 | tf_op jit(solution)/shard_map/dot_general | solution.py:65
  298.0 1.6 copy.98
  299.6 4.8 %all-to-all-start.2 = ((bf16[4,256,1024]{2,1,0:T(8,128)(2,1)}), bf16[4,256,1024]{2,1,0:T(8,128)(2,1)}, u32[]{:S(2)}, u32[]{:S(2)}) async-start(bf16[4,256,1024]{2,1,0:T(8,128)(2,1)} %bitcast.100), calls=%async_computation.2 | async-start | bytes 4194304 | tf_op jit(solution)/shard_map/all_to_all | solution.py:51
  304.6 0.3 reshape.137
  304.9 0.4 convolution_convert_fusion.1
  305.3 1.0 collective-permute-start.6
  306.3 0.4 convolution_convert_fusion.2
  306.7 0.4 convolution_convert_fusion
  307.1 0.4 convolution_convert_fusion.3
  307.4 1.3 collective-permute-start.5
  308.7 1.3 collective-permute-start.7
  310.0 2.1 collective-permute-start.4
  312.2 0.3 fusion.68
  312.5 1.7 collective-permute-done.5
  314.2 0.3 fusion.71
  314.6 3.0 collective-permute-done.7
  317.5 0.3 fusion.65
  317.9 0.7 collective-permute-done.4
  318.6 0.3 fusion.7
  318.9 0.3 reshape.138
  319.2 0.8 copy.55
  320.0 10.6 %all-to-all-done.2 = bf16[4,256,1024]{2,1,0:T(8,128)(2,1)} async-done(((bf16[4,256,1024]{2,1,0:T(8,128)(2,1)}), bf16[4,256,1024]{2,1,0:T(8,128)(2,1)}, u32[]{:S(2)}, u32[]{:S(2)}) %all-to-all-start.2) | async-done | bytes 2097184 | tf_op jit(solution)/shard_map/all_to_all | solution.py:51
  330.6 2.0 reduce.1
  332.6 0.8 fusion.114
  (39 shorter events, 2.4 us)
Async XLA Ops:
  7.2 52.8 %copy-start = (bf16[768,1024]{1,0:T(8,128)(2,1)S(1)}, bf16[768,1024]{1,0:T(8,128)(2,1)}, u32[]{:S(2)}) copy-start(bf16[768,1024]{1,0:T(8,128)(2,1)} %param.12) | copy-start | bytes 4718596
  7.2 15.3 %copy-start.7 = (s32[1,4]{1,0:T(1,128)S(1)}, s32[1,4]{1,0:T(1,128)}, u32[]{:S(2)}) copy-start(s32[1,4]{1,0:T(1,128)} %param.16) | copy-start | bytes 52
  9.6 12.9 %collective-permute-start.1 = (bf16[2,24576]{1,0:T(2,128)(2,1)S(1)}, bf16[2,24576]{1,0:T(2,128)(2,1)S(1)}, u32[]{:S(2)}, u32[]{:S(2)}) collective-permute-start(bf16[2,24576]{1,0:T(2,128)(2,1)S(1)} %convolution_convert_fusion.6), channel_id=1, source_target_pairs={{0,248},{4,252},{8,0},{12,4},{16,8},{20,12},{24,16},{28,20},{32,24... | collective-permute-start | bytes 294920 | tf_op jit(solution)/shard_map/ppermute | solution.py:25
  12.3 10.5 %collective-permute-start.2 = (bf16[2,24576]{1,0:T(2,128)(2,1)S(1)}, bf16[2,24576]{1,0:T(2,128)(2,1)S(1)}, u32[]{:S(2)}, u32[]{:S(2)}) collective-permute-start(bf16[2,24576]{1,0:T(2,128)(2,1)S(1)} %convolution_convert_fusion.5), channel_id=1, source_target_pairs={{0,244},{4,248},{8,252},{12,0},{16,4},{20,8},{24,12},{28,16},{32,2... | collective-permute-start | bytes 294920 | tf_op jit(solution)/shard_map/ppermute | solution.py:25
  12.6 10.5 %collective-permute-start.3 = (bf16[2,24576]{1,0:T(2,128)(2,1)S(1)}, bf16[2,24576]{1,0:T(2,128)(2,1)S(1)}, u32[]{:S(2)}, u32[]{:S(2)}) collective-permute-start(bf16[2,24576]{1,0:T(2,128)(2,1)S(1)} %convolution_convert_fusion.4), channel_id=1, source_target_pairs={{0,240},{4,244},{8,248},{12,252},{16,0},{20,4},{24,8},{28,12},{32,... | collective-permute-start | bytes 294920 | tf_op jit(solution)/shard_map/ppermute | solution.py:25
  20.9 3.7 %collective-permute-start = (bf16[2,24576]{1,0:T(2,128)(2,1)S(1)}, bf16[2,24576]{1,0:T(2,128)(2,1)S(1)}, u32[]{:S(2)}, u32[]{:S(2)}) collective-permute-start(bf16[2,24576]{1,0:T(2,128)(2,1)S(1)} %convolution_convert_fusion.7), channel_id=1, source_target_pairs={{0,252},{4,0},{8,4},{12,8},{16,12},{20,16},{24,20},{28,24},{32,28}... | collective-permute-start | bytes 294920 | tf_op jit(solution)/shard_map/ppermute | solution.py:25
  25.0 15.1 %copy-start.6 = (bf16[1024,64]{0,1:T(8,128)(2,1)S(1)}, bf16[1024,64]{0,1:T(8,128)(2,1)}, u32[]{:S(2)}) copy-start(bf16[1024,64]{0,1:T(8,128)(2,1)} %param.14) | copy-start | bytes 393220
  44.4 11.1 %copy-start.4 = (bf16[128,1024]{1,0:T(8,128)(2,1)S(1)}, bf16[128,1024]{1,0:T(8,128)(2,1)}, u32[]{:S(2)}) copy-start(bf16[128,1024]{1,0:T(8,128)(2,1)} %param.10) | copy-start | bytes 786436
  44.4 11.1 %copy-start.5 = (bf16[128,1024]{1,0:T(8,128)(2,1)S(1)}, bf16[128,1024]{1,0:T(8,128)(2,1)}, u32[]{:S(2)}) copy-start(bf16[128,1024]{1,0:T(8,128)(2,1)} %param.9) | copy-start | bytes 786436
  44.4 197.1 %all-to-all-start.1 = ((bf16[64,1024,64]{1,2,0:T(8,128)(2,1)}), bf16[64,1024,64]{1,2,0:T(8,128)(2,1)}, u32[]{:S(2)}, u32[]{:S(2)}) async-start(bf16[64,1024,64]{1,2,0:T(8,128)(2,1)} %stack.2), calls=%async_computation.1 | async-start | bytes 16777216 | tf_op jit(solution)/shard_map/all_to_all | solution.py:89
  55.2 35.4 %all-gather.2.cloned.1.call-start = ((), (), s32[]{:S(2)}) async-start(), calls=%async_computation.4 | async-start | bytes 2621440 | tf_op jit(solution)/shard_map/all_gather | solution.py:16
  96.1 1.0 copy-start.2
  241.5 5.1 %copy-start.1 = (bf16[64,8,8,128]{3,2,1,0:T(8,128)(2,1)S(1)}, bf16[64,8,8,128]{3,2,1,0:T(8,128)(2,1)}, u32[]{:S(2)}) copy-start(bf16[64,8,8,128]{3,2,1,0:T(8,128)(2,1)} %copy.59) | copy-start | bytes 3145732
  272.1 3.6 %copy-start.3 = (bf16[2,256,8,128]{1,3,2,0:T(8,128)(2,1)S(1)}, bf16[2,256,8,128]{1,3,2,0:T(8,128)(2,1)}, u32[]{:S(2)}) copy-start(bf16[2,256,8,128]{1,3,2,0:T(8,128)(2,1)} %fusion.12) | copy-start | bytes 3145732
  281.6 18.0 %all-to-all-start.3 = ((bf16[4,512,192]{1,2,0:T(8,128)(2,1)}), bf16[4,512,192]{1,2,0:T(8,128)(2,1)S(1)}, u32[]{:S(2)}, u32[]{:S(2)}) async-start(bf16[4,512,192]{1,2,0:T(8,128)(2,1)} %bitcast.17), calls=%async_computation.3 | async-start | bytes 1572864 | tf_op jit(solution)/shard_map/all_to_all | solution.py:51
  299.6 31.0 %all-to-all-start.2 = ((bf16[4,256,1024]{2,1,0:T(8,128)(2,1)}), bf16[4,256,1024]{2,1,0:T(8,128)(2,1)}, u32[]{:S(2)}, u32[]{:S(2)}) async-start(bf16[4,256,1024]{2,1,0:T(8,128)(2,1)} %bitcast.100), calls=%async_computation.2 | async-start | bytes 4194304 | tf_op jit(solution)/shard_map/all_to_all | solution.py:51
  305.3 6.9 %collective-permute-start.6 = (bf16[2,24576]{1,0:T(2,128)(2,1)S(1)}, bf16[2,24576]{1,0:T(2,128)(2,1)S(1)}, u32[]{:S(2)}, u32[]{:S(2)}) collective-permute-start(bf16[2,24576]{1,0:T(2,128)(2,1)S(1)} %convolution_convert_fusion.1), channel_id=1, source_target_pairs={{0,12},{4,16},{8,20},{12,24},{16,28},{20,32},{24,36},{28,40},{32,4... | collective-permute-start | bytes 294920 | tf_op jit(solution)/shard_map/ppermute | solution.py:25
  307.4 6.8 %collective-permute-start.5 = (bf16[2,24576]{1,0:T(2,128)(2,1)S(1)}, bf16[2,24576]{1,0:T(2,128)(2,1)S(1)}, u32[]{:S(2)}, u32[]{:S(2)}) collective-permute-start(bf16[2,24576]{1,0:T(2,128)(2,1)S(1)} %convolution_convert_fusion.2), channel_id=1, source_target_pairs={{0,8},{4,12},{8,16},{12,20},{16,24},{20,28},{24,32},{28,36},{32,40... | collective-permute-start | bytes 294920 | tf_op jit(solution)/shard_map/ppermute | solution.py:25
  308.7 8.8 %collective-permute-start.7 = (bf16[2,24576]{1,0:T(2,128)(2,1)S(1)}, bf16[2,24576]{1,0:T(2,128)(2,1)S(1)}, u32[]{:S(2)}, u32[]{:S(2)}) collective-permute-start(bf16[2,24576]{1,0:T(2,128)(2,1)S(1)} %convolution_convert_fusion), channel_id=1, source_target_pairs={{0,16},{4,20},{8,24},{12,28},{16,32},{20,36},{24,40},{28,44},{32,4... | collective-permute-start | bytes 294920 | tf_op jit(solution)/shard_map/ppermute | solution.py:25
  310.0 8.6 %collective-permute-start.4 = (bf16[2,24576]{1,0:T(2,128)(2,1)S(1)}, bf16[2,24576]{1,0:T(2,128)(2,1)S(1)}, u32[]{:S(2)}, u32[]{:S(2)}) collective-permute-start(bf16[2,24576]{1,0:T(2,128)(2,1)S(1)} %convolution_convert_fusion.3), channel_id=1, source_target_pairs={{0,4},{4,8},{8,12},{12,16},{16,20},{20,24},{24,28},{28,32},{32,36}... | collective-permute-start | bytes 294920 | tf_op jit(solution)/shard_map/ppermute | solution.py:25
Sparse Core Ops, SparseCore 0:
  57.9 32.6 all-gather.1
